TPU v7x, 256 devices: a whole 4x4x8 slice. The times are simulated.
256 devices in a mesh: pair: 64 (over y, z, core), row: 4 (over x).
Axes of the slice: x: 4, y: 4, z: 8, core: 2. Of those that a mesh axis runs over, the one named last changes fastest.
Arguments:
- whitened: float32 [4096, 16384], P('row', 'pair'), may hold values from -50 to 50, as said below
- offsets: int32 [4, 4], replicated, may hold values from 0 to 127
Outputs:
- rotated: float32 [4096, 16384], P('row', 'pair')
- right_vectors: float32 [16384, 16384], P('row', 'pair')
Inputs may be any that keep to these rules, and one draw needn't show every extreme that they name: whitened has rows and columns of different scales.
All inputs are finite; a program needn't handle non-finite values.
Results may differ from a plain program's by a relative error of at most 0.0003.
Values sent between devices are 32-bit elements; how exact they have to be, the bound alone decides.
A program may use at most 64 MiB of HBM per device.

v0:
```python
import functools

import jax
import jax.numpy as jnp
from jax import lax
from jax.experimental import pallas as pl
from jax.experimental.pallas import tpu as pltpu
from jax.sharding import PartitionSpec as P

B = 128
WIDTH = 2 * B
ROUNDS = 4
STEPS = 4
CHUNKS = 4
SETS = 14
ROWS_SENT = 4 * SETS
MESH = pl.DeviceIdType.MESH
F32 = jnp.float32

KEPT = [
    ([0, 1, 2, 3, 4], [5, 6, 7, 8, 9], [None, 10, 11, 12, 13]),
    ([0, 2], [1, 3], [None, 4]),
    ([0], [1], [None]),
]


def gram(x):
    return lax.dot_general(x, x, (((0,), (0,)), ((), ())), precision=lax.Precision.HIGHEST, preferred_element_type=F32)


def ahead(x, by):
    return pltpu.roll(x, lax.rem(B - by, B), 1)


def turns(offs_ref, step):
    offs = [offs_ref[step, r] for r in range(ROUNDS)]
    before = [jnp.int32(0)] + offs[:-1]
    return [lax.rem(b - o + B, B) for b, o in zip(before, offs)], offs[-1]


def distances(offs_ref, step):
    o = [offs_ref[step, r] for r in range(ROUNDS)]
    d1, d2, d3 = [lax.rem(b - a + B, B) for a, b in zip(o, o[1:])]
    near = [jnp.int32(0), d2, d3, d3 + d2, d3 - d2]
    far = near + [e + d1 for e in near] + [e - d1 for e in near[1:]]
    far = [lax.rem(e + 2 * B, B) for e in far]
    return o[0], (d1, d2, d3), [far, far[:5], [far[0], far[2]]]


def pick_diagonals(total, w_ref, dst_ref, offs_ref, step):
    o, _, far = distances(offs_ref, step)
    w_ref[0] = total[B:, B:]
    w_ref[1] = total[:B, B:]
    w_ref[2] = total[:B, :B]
    w_ref[3] = total[B:, :B]
    base = lax.broadcasted_iota(jnp.int32, (8, B), 0) - lax.broadcasted_iota(jnp.int32, (8, B), 1)
    for q in range(4):
        at = [lax.rem(e - o + B, B) if q == 1 else lax.rem(e + o, B) if q == 3 else e for e in far[0]]
        acc = [jnp.zeros((8, B), F32) for _ in at]
        for g in range(B // 8):
            m = w_ref[q, 8 * g : 8 * g + 8, :]
            dist = (base + 8 * g) & (B - 1)
            acc = [jnp.where(dist == t, m, v) for t, v in zip(at, acc)]
        for i, v in enumerate(acc):
            dst_ref[pl.ds(q * SETS + i, 1), :] = jnp.sum(v, axis=0, keepdims=True)
    dst_ref[pl.ds(0, 2 * SETS), :] = ahead(dst_ref[pl.ds(0, 2 * SETS), :], o)


def solve_angles(t_ref, offs_ref, step, cs_ref):
    _, turn, far = distances(offs_ref, step)
    d, e, a, b = [[t_ref[pl.ds(q * SETS + i, 1), :] for i in range(SETS)] for q in range(4)]
    for r in range(ROUNDS):
        gap = 0.5 * (d[0] - a[0])
        c0 = b[0]
        radius = jnp.sqrt(gap * gap + c0 * c0)
        sign = jnp.where(gap >= 0, 1.0, -1.0)
        t = -sign * c0 / (jnp.abs(gap) + radius + 1e-06 * (a[0] + d[0]))
        c = 1.0 / jnp.sqrt(1.0 + t * t)
        s = t * c
        cs_ref[pl.ds(r, 1), :] = c
        cs_ref[pl.ds(ROUNDS + r, 1), :] = s
        if r == ROUNDS - 1:
            break

        def partner(i):
            return (c, s) if i == 0 else (ahead(c, far[r][i]), ahead(s, far[r][i]))

        na, nb, nd, ne = [], [], [], []
        for i in KEPT[r][0]:
            cc, ss = partner(i)
            u1, u2 = cc * a[i] + ss * b[i], cc * e[i] + ss * d[i]
            v1, v2 = cc * b[i] - ss * a[i], cc * d[i] - ss * e[i]
            na.append(c * u1 + s * u2)
            nd.append(ahead(c * v2 - s * v1, turn[r]))
        for i in KEPT[r][1]:
            cc, ss = partner(i)
            v1, v2 = cc * b[i] - ss * a[i], cc * d[i] - ss * e[i]
            nb.append(c * v1 + s * v2)
        for i in KEPT[r][2]:
            if i is None:
                ne.append(nb[0])
                continue
            cc, ss = partner(i)
            u1, u2 = cc * a[i] + ss * b[i], cc * e[i] + ss * d[i]
            ne.append(ahead(c * u2 - s * u1, turn[r]))
        a, b, d, e = na, nb, nd, ne


def rotated(f, s, cs_ref, turn):
    shifts, back = turn
    for r in range(ROUNDS):
        s = pltpu.roll(s, shifts[r], 1)
        c = cs_ref[pl.ds(r, 1), :]
        n = cs_ref[pl.ds(ROUNDS + r, 1), :]
        f, s = f * c + s * n, s * c - f * n
    return f, pltpu.roll(s, back, 1)


def main_kernel(
    n_pair, n_row, rows, offs_hbm, x_hbm, x_out, w_out,
    offs_ref, x_in, xf, xs, of, os_, w_ref, gs, tot, cs, hl, hr, le, re,
    r0l, l0l, r0r, l0r, r1, l1, edge0, edge1, w3f, w3s,
    in_sem, g_send, g_recv, x_send, x_recv, h_send, h_recv,
):
    k = lax.axis_index("pair")
    me = lax.axis_index("row")
    first, last = k == 0, k == n_pair - 1
    chunk = rows // CHUNKS

    fetch_offs = pltpu.make_async_copy(offs_hbm, offs_ref, in_sem.at[CHUNKS])
    fetch_offs.start()
    fetch = [
        pltpu.make_async_copy(x_hbm.at[pl.ds(c * chunk, chunk)], x_in.at[pl.ds(c * chunk, chunk)], in_sem.at[c])
        for c in range(CHUNKS)
    ]
    for copy in fetch:
        copy.start()

    barrier = pltpu.get_barrier_semaphore()

    @pl.when(k > 0)
    def _():
        pl.semaphore_signal(barrier, inc=1, device_id={"pair": k - 1}, device_id_type=MESH)

    @pl.when(k < n_pair - 1)
    def _():
        pl.semaphore_signal(barrier, inc=1, device_id={"pair": k + 1}, device_id_type=MESH)

    for j in range(1, n_row):
        pl.semaphore_signal(barrier, inc=1, device_id={"row": lax.rem(me + j, n_row)}, device_id_type=MESH)

    def to_right(src, dst, sems, at):
        return pltpu.make_async_remote_copy(
            src_ref=src, dst_ref=dst, send_sem=sems[0].at[(0,) + at], recv_sem=sems[1].at[(0,) + at],
            device_id={"pair": k + 1}, device_id_type=MESH,
        )

    def to_left(src, dst, sems, at):
        return pltpu.make_async_remote_copy(
            src_ref=src, dst_ref=dst, send_sem=sems[0].at[(1,) + at], recv_sem=sems[1].at[(1,) + at],
            device_id={"pair": k - 1}, device_id_type=MESH,
        )

    def arrived(dst_l, dst_r, sems, at):
        @pl.when(k > 0)
        def _():
            to_right(dst_l, dst_l, sems, at).wait_recv()

        @pl.when(k < n_pair - 1)
        def _():
            to_left(dst_r, dst_r, sems, at).wait_recv()

    def sent(src_r, src_l, sems, at):
        @pl.when(k < n_pair - 1)
        def _():
            to_right(src_r, src_r, sems, at).wait_send()

        @pl.when(k > 0)
        def _():
            to_left(src_l, src_l, sems, at).wait_send()

    def peer_copy(step, slot, to):
        return pltpu.make_async_remote_copy(
            src_ref=gs.at[step, slot], dst_ref=gs.at[step, slot], send_sem=g_send.at[step, to],
            recv_sem=g_recv.at[step, slot], device_id={"row": to}, device_id_type=MESH,
        )

    x_sems, h_sems = (x_send, x_recv), (h_send, h_recv)

    def send_rows(step, c):
        at = pl.ds(c * chunk, chunk)
        f, s = of.at[step, at], os_.at[step, at]
        new_f, new_s = xf.at[step, at], xs.at[step, at]

        @pl.when(first)
        def _():
            to_right(s, new_f, x_sems, (step, c)).start()
            new_f[...] = f[...]

        @pl.when(jnp.logical_and(k > 0, k < n_pair - 1))
        def _():
            to_right(f, new_f, x_sems, (step, c)).start()

        @pl.when(last)
        def _():
            new_s[...] = f[...]

        @pl.when(k > 0)
        def _():
            to_left(s, new_s, x_sems, (step, c)).start()

    def send_history(step):
        if step > 0:
            le[step, pl.ds(0, step)] = hl[step - 1, pl.ds(0, step)]
            re[step, pl.ds(0, step)] = hr[step - 1, pl.ds(0, step)]
        le[step, step] = cs[step]
        re[step, step] = cs[step]
        n = pl.ds(0, step + 1)

        @pl.when(k < n_pair - 1)
        def _():
            to_right(le.at[step, n], hl.at[step, n], h_sems, (step,)).start()

        @pl.when(k > 0)
        def _():
            to_left(re.at[step, n], hr.at[step, n], h_sems, (step,)).start()

        @pl.when(first)
        def _():
            hl[step, n] = re[step, n]

        @pl.when(last)
        def _():
            hr[step, n] = le[step, n]

    def history_arrived(step):
        n = pl.ds(0, step + 1)
        arrived(hl.at[step, n], hr.at[step, n], h_sems, (step,))

    def node(level, slot, cs_ref, from_left, from_right, dst_right, dst_left):
        turn = turns(offs_ref, level)
        outside = jnp.logical_or(slot < 0, slot >= n_pair)
        swap = jnp.logical_or(jnp.logical_or(slot < -1, slot == 0), slot >= n_pair)
        for g in range(level + 1):
            at = pl.ds(g * WIDTH, WIDTH)
            if level == 0:
                row = lax.broadcasted_iota(jnp.int32, (WIDTH, B), 0)
                col = lax.broadcasted_iota(jnp.int32, (WIDTH, B), 1)
                f, s = [jnp.where(row == col + h, 1.0, 0.0).astype(F32) for h in (0, B)]
            else:
                zero = jnp.zeros((WIDTH, B), F32)
                p = from_left[at, :] if g < level else zero
                q = from_right[pl.ds((g - 1) * WIDTH, WIDTH), :] if g > 0 else zero
                f, s = jnp.where(outside, q, p), jnp.where(outside, p, q)
            f, s = rotated(f, s, cs_ref, turn)
            if dst_right is not None:
                dst_right[at, :] = jnp.where(swap, s, f)
            if dst_left is not None:
                dst_left[at, :] = jnp.where(swap, f, s)

    total = jnp.zeros((WIDTH, WIDTH), F32)
    for c in range(CHUNKS):
        fetch[c].wait()
        total = total + gram(x_in[pl.ds(c * chunk, chunk), :])
    fetch_offs.wait()
    for step in range(STEPS):
        if step > 0:
            history_arrived(step - 1)
            if step == 1:
                node(0, k - 1, hl.at[0, 0], None, None, r0l, l0l)
                node(0, k + 1, hr.at[0, 0], None, None, r0r, l0r)
            if step == 2:
                node(1, k, cs.at[1], r0l, l0r, r1, l1)
            if step == 3:
                node(0, k - 3, hl.at[2, 0], None, None, edge0, None)
                node(1, k - 2, hl.at[2, 1], edge0, l0l, edge1, None)
                node(2, k - 1, hl.at[2, 2], edge1, l1, w3f, None)
                node(0, k + 3, hr.at[2, 0], None, None, None, edge0)
                node(1, k + 2, hr.at[2, 1], r0r, edge0, None, edge1)
                node(2, k + 1, hr.at[2, 2], r1, edge1, None, w3s)
            total = jnp.zeros((WIDTH, WIDTH), F32)
            for c in range(CHUNKS):
                at = pl.ds(c * chunk, chunk)
                arrived(xf.at[step - 1, at], xs.at[step - 1, at], x_sems, (step - 1, c))
                total = total + gram(jnp.concatenate([xf[step - 1, at, :], xs[step - 1, at, :]], axis=1))
        pick_diagonals(total, w_ref, gs.at[step, me], offs_ref, step)
        if step == 0:
            pl.semaphore_wait(barrier, n_row - 1 + (k > 0).astype(jnp.int32) + (k < n_pair - 1).astype(jnp.int32))
        for j in range(1, n_row):
            peer_copy(step, me, lax.rem(me + j, n_row)).start()
        for j in range(1, n_row):
            peer_copy(step, lax.rem(me + j, n_row), lax.rem(me + j, n_row)).wait_recv()
        tot[...] = sum((gs[step, i] for i in range(1, n_row)), gs[step, 0])
        solve_angles(tot, offs_ref, step, cs.at[step])
        turn = turns(offs_ref, step)
        if step < STEPS - 1:
            send_history(step)
        for c in range(CHUNKS):
            at = pl.ds(c * chunk, chunk)
            if step == 0:
                f, s = x_in[at, :B], x_in[at, B:]
            else:
                f, s = xf[step - 1, at, :], xs[step - 1, at, :]
            f, s = rotated(f, s, cs.at[step], turn)
            if step < STEPS - 1:
                of[step, at, :] = f
                os_[step, at, :] = s
                send_rows(step, c)
            else:
                x_out[at, :B] = f
                x_out[at, B:] = s

    turn = turns(offs_ref, STEPS - 1)
    for g in range(STEPS):
        at = pl.ds(g * WIDTH, WIDTH)
        zero = jnp.zeros((WIDTH, B), F32)
        f = w3f[at, :] if g < STEPS - 1 else zero
        s = w3s[pl.ds((g - 1) * WIDTH, WIDTH), :] if g > 0 else zero
        f, s = rotated(f, s, cs.at[STEPS - 1], turn)
        w_out[at, :B] = f
        w_out[at, B:] = s

    for step in range(STEPS):
        for j in range(1, n_row):
            peer_copy(step, me, lax.rem(me + j, n_row)).wait_send()
        if step < STEPS - 1:
            n = pl.ds(0, step + 1)
            sent(le.at[step, n], re.at[step, n], h_sems, (step,))
            for c in range(CHUNKS):
                at = pl.ds(c * chunk, chunk)
                sent(of.at[step, at], os_.at[step, at], x_sems, (step, c))


def place_kernel(n_pair, blocks, x_ref, w_ref, x_out, v_out, zero, sem):
    k, me = lax.axis_index("pair"), lax.axis_index("row")
    move_x = pltpu.make_async_copy(x_ref, x_out, sem.at[blocks + STEPS])
    move_x.start()
    zero[...] = jnp.zeros_like(zero)
    slots = []
    for j in range(STEPS):
        slot = k - (STEPS - 1) + 2 * j
        slot = jnp.where(slot < 0, -1 - slot, slot)
        slots.append(jnp.where(slot >= n_pair, 2 * n_pair - 1 - slot, slot) - me * blocks)

    def piece(j):
        here = jnp.logical_and(slots[j] >= 0, slots[j] < blocks)
        place = pl.multiple_of(jnp.where(here, slots[j], 0) * WIDTH, WIDTH)
        return here, pltpu.make_async_copy(
            w_ref.at[pl.ds(j * WIDTH, WIDTH)], v_out.at[pl.ds(place, WIDTH)], sem.at[blocks + j]
        )

    def blank(b):
        empty = slots[0] != b
        for j in range(1, STEPS):
            empty = jnp.logical_and(empty, slots[j] != b)
        return empty, pltpu.make_async_copy(zero, v_out.at[pl.ds(b * WIDTH, WIDTH)], sem.at[b])

    moves = [piece(j) for j in range(STEPS)] + [blank(b) for b in range(blocks)]
    for needed, copy in moves:
        pl.when(needed)(copy.start)
    for needed, copy in moves:
        pl.when(needed)(copy.wait)
    move_x.wait()


def body(n_pair, n_row, whitened, offsets):
    rows, width = whitened.shape
    v_rows = n_pair * width // n_row
    blocks = v_rows // width
    sds = functools.partial(jax.ShapeDtypeStruct, dtype=F32)
    vmem = pl.BlockSpec(memory_space=pltpu.VMEM)
    anywhere = pl.BlockSpec(memory_space=pl.ANY)
    dma = pltpu.SemaphoreType.DMA

    def held(*shape):
        return pltpu.VMEM(shape, F32)

    x_last, w_last = pl.pallas_call(
        functools.partial(main_kernel, n_pair, n_row, rows),
        out_shape=[sds((rows, width)), sds((STEPS * width, width))],
        in_specs=[anywhere, anywhere],
        out_specs=[vmem, vmem],
        scratch_shapes=[
            pltpu.SMEM((STEPS, ROUNDS), jnp.int32),
            held(rows, width),
            held(STEPS - 1, rows, B),
            held(STEPS - 1, rows, B),
            held(STEPS - 1, rows, B),
            held(STEPS - 1, rows, B),
            held(4, B, B),
            held(STEPS, n_row, ROWS_SENT, B),
            held(ROWS_SENT, B),
            held(STEPS, 2 * ROUNDS, B),
        ]
        + [held(STEPS - 1, STEPS - 1, 2 * ROUNDS, B) for _ in range(4)]
        + [held(n * width, B) for n in (1, 1, 1, 1, 2, 2, 1, 2, 3, 3)]
        + [
            dma((CHUNKS + 1,)),
            dma((STEPS, n_row)),
            dma((STEPS, n_row)),
            dma((2, STEPS - 1, CHUNKS)),
            dma((2, STEPS - 1, CHUNKS)),
            dma((2, STEPS - 1)),
            dma((2, STEPS - 1)),
        ],
        compiler_params=pltpu.CompilerParams(
            collective_id=0, has_side_effects=True, vmem_limit_bytes=40 * 1024 * 1024
        ),
    )(offsets, whitened)
    return pl.pallas_call(
        functools.partial(place_kernel, n_pair, blocks),
        out_shape=[sds((rows, width)), sds((v_rows, width))],
        in_specs=[vmem, vmem],
        out_specs=[anywhere, anywhere],
        scratch_shapes=[held(width, width), dma((blocks + STEPS + 1,))],
    )(x_last, w_last)


def solution(mesh):
    n_pair, n_row = mesh.shape["pair"], mesh.shape["row"]
    return jax.shard_map(
        functools.partial(body, n_pair, n_row),
        mesh=mesh,
        in_specs=(P("row", "pair"), P()),
        out_specs=(P("row", "pair"), P("row", "pair")),
        check_vma=False,
    )
```

profile of v0, /device:TPU:24, one launch (start us, length us, event | category | flops | bytes accessed | tf_op | source)
XLA Modules:
  0.0 64.5 jit_solution(11562006102156018367)
XLA Ops:
  0.6 0.0 copy-start
  0.6 1.2 %copy-done = f32[1024,256]{1,0:T(8,128)S(1)} copy-done((f32[1024,256]{1,0:T(8,128)S(1)}, f32[1024,256]{1,0:T(8,128)}, u32[]{:S(2)}) %copy-start) | copy-done | bytes 1048600
  1.9 0.0 copy-start.3
  1.9 0.7 %copy-done.3 = s32[4,4]{1,0:T(4,128)S(1)} copy-done((s32[4,4]{1,0:T(4,128)S(1)}, s32[4,4]{1,0:T(4,128)}, u32[]{:S(2)}) %copy-start.3) | copy-done | bytes 88
  2.5 55.8 %shard_map.41 = (f32[1024,256]{1,0:T(8,128)S(1)}, f32[1024,256]{1,0:T(8,128)S(1)}) custom-call(s32[4,4]{1,0:T(4,128)S(1)} %copy-done.3, f32[1024,256]{1,0:T(8,128)S(1)} %copy-done), custom_call_target="tpu_custom_call" | custom-call | tf_op jit(solution)/shard_map/pallas_call | solution.py:378
  58.3 0.0 copy-start.1
  58.3 1.0 %copy-done.1 = f32[1024,256]{1,0:T(8,128)} copy-done((f32[1024,256]{1,0:T(8,128)}, f32[1024,256]{1,0:T(8,128)S(1)}, u32[]{:S(2)}) %copy-start.1) | copy-done | bytes 1048600
  59.3 0.0 copy-start.2
  59.3 1.0 %copy-done.2 = f32[1024,256]{1,0:T(8,128)} copy-done((f32[1024,256]{1,0:T(8,128)}, f32[1024,256]{1,0:T(8,128)S(1)}, u32[]{:S(2)}) %copy-start.2) | copy-done | bytes 1048600
  60.3 4.0 %shard_map.42 = (f32[1024,256]{1,0:T(8,128)}, f32[4096,256]{1,0:T(8,128)}) custom-call(f32[1024,256]{1,0:T(8,128)} %copy-done.1, f32[1024,256]{1,0:T(8,128)} %copy-done.2), custom_call_target="tpu_custom_call" | custom-call | tf_op jit(solution)/shard_map/pallas_call | solution.py:410
Async XLA Ops:
  0.6 1.2 %copy-start = (f32[1024,256]{1,0:T(8,128)S(1)}, f32[1024,256]{1,0:T(8,128)}, u32[]{:S(2)}) copy-start(f32[1024,256]{1,0:T(8,128)} %x_hbm.1) | copy-start | bytes 3145732
  1.9 0.7 %copy-start.3 = (s32[4,4]{1,0:T(4,128)S(1)}, s32[4,4]{1,0:T(4,128)}, u32[]{:S(2)}) copy-start(s32[4,4]{1,0:T(4,128)} %offs_hbm.1) | copy-start | bytes 196
  58.3 1.0 %copy-start.1 = (f32[1024,256]{1,0:T(8,128)}, f32[1024,256]{1,0:T(8,128)S(1)}, u32[]{:S(2)}) copy-start(f32[1024,256]{1,0:T(8,128)S(1)} %get-tuple-element.4.x_ref) | copy-start | bytes 3145732
  59.3 1.0 %copy-start.2 = (f32[1024,256]{1,0:T(8,128)}, f32[1024,256]{1,0:T(8,128)S(1)}, u32[]{:S(2)}) copy-start(f32[1024,256]{1,0:T(8,128)S(1)} %get-tuple-element.5.w_ref) | copy-start | bytes 3145732
where the time goes:
time: 64.7 us; the launch traced here: 64.5 us
  Pallas kernels  59.8 us (92%)
  local copies, waits for them, and re-layouts  3.87 us (6%)
  between operations  0.82 us (1%)
    pallas_call x1, Pallas kernels, body(): pl.pallas_call(functools.partial(main_kernel, n_pair, n_row, rows), out_s...  55.8 us
    pallas_call x1, Pallas kernels, body(): pl.pallas_call(functools.partial(place_kernel, n_pair, blocks), out_shape...  4.04 us
    unnamed x8, local copies, waits for them, and re-layouts  3.87 us

commit v1 on v0

--- a/solution.py
+++ b/solution.py
@@ -11,7 +11,9 @@
 WIDTH = 2 * B
 ROUNDS = 4
 STEPS = 4
-CHUNKS = 4
+FETCHES = 4
+LATE = 3
+EARLY = 7
 SETS = 14
 ROWS_SENT = 4 * SETS
 MESH = pl.DeviceIdType.MESH
@@ -117,21 +119,23 @@
 
 
 def main_kernel(
-    n_pair, n_row, rows, offs_hbm, x_hbm, x_out, w_out,
-    offs_ref, x_in, xf, xs, of, os_, w_ref, gs, tot, cs, hl, hr, le, re,
+    n_pair, n_row, rows, early, offs_hbm, x_hbm, x_out, w_out,
+    offs_ref, x_in, xf, xs, of, os_, el, er, w_ref, gs, tot, cs, hl, hr, le, re,
     r0l, l0l, r0r, l0r, r1, l1, edge0, edge1, w3f, w3s,
-    in_sem, g_send, g_recv, x_send, x_recv, h_send, h_recv,
+    in_sem, g_send, g_recv, x_send, x_recv, e_send, e_recv, h_send, h_recv,
 ):
     k = lax.axis_index("pair")
     me = lax.axis_index("row")
     first, last = k == 0, k == n_pair - 1
-    chunk = rows // CHUNKS
-
-    fetch_offs = pltpu.make_async_copy(offs_hbm, offs_ref, in_sem.at[CHUNKS])
+    piece = rows // FETCHES
+    late = (rows - early) // LATE
+    top = pl.ds(0, early)
+
+    fetch_offs = pltpu.make_async_copy(offs_hbm, offs_ref, in_sem.at[FETCHES])
     fetch_offs.start()
     fetch = [
-        pltpu.make_async_copy(x_hbm.at[pl.ds(c * chunk, chunk)], x_in.at[pl.ds(c * chunk, chunk)], in_sem.at[c])
-        for c in range(CHUNKS)
+        pltpu.make_async_copy(x_hbm.at[pl.ds(c * piece, piece)], x_in.at[pl.ds(c * piece, piece)], in_sem.at[c])
+        for c in range(FETCHES)
     ]
     for copy in fetch:
         copy.start()
@@ -185,10 +189,13 @@
             recv_sem=g_recv.at[step, slot], device_id={"row": to}, device_id_type=MESH,
         )
 
-    x_sems, h_sems = (x_send, x_recv), (h_send, h_recv)
-
-    def send_rows(step, c):
-        at = pl.ds(c * chunk, chunk)
+    x_sems, e_sems, h_sems = (x_send, x_recv), (e_send, e_recv), (h_send, h_recv)
+
+    def late_rows(c):
+        return pl.ds(early + c * late, late)
+
+    def send_late(step, c):
+        at = late_rows(c)
         f, s = of.at[step, at], os_.at[step, at]
         new_f, new_s = xf.at[step, at], xs.at[step, at]
 
@@ -208,6 +215,38 @@
         @pl.when(k > 0)
         def _():
             to_left(s, new_s, x_sems, (step, c)).start()
+
+    def early_source(step, h):
+        if step == 0:
+            return x_in.at[top, pl.ds(h * B, B)]
+        return (xf, xs)[h].at[step - 1, top]
+
+    def send_early(step):
+        for h in range(2):
+            src = early_source(step, h)
+
+            @pl.when(k < n_pair - 1)
+            def _():
+                to_right(src, el.at[step, h], e_sems, (step, h)).start()
+
+            @pl.when(k > 0)
+            def _():
+                to_left(src, er.at[step, h], e_sems, (step, h)).start()
+
+            @pl.when(first)
+            def _():
+                el[step, h] = src[...]
+
+            @pl.when(last)
+            def _():
+                er[step, h] = src[...]
+
+    def rotate_early(step):
+        turn = turns(offs_ref, step)
+        f, s = rotated(el[step, 0], el[step, 1], hl.at[step, step], turn)
+        xf[step, top, :] = jnp.where(k == 1, s, f)
+        f, s = rotated(er[step, 0], er[step, 1], hr.at[step, step], turn)
+        xs[step, top, :] = jnp.where(last, f, s)
 
     def send_history(step):
         if step > 0:
@@ -233,89 +272,94 @@
         def _():
             hr[step, n] = le[step, n]
 
-    def history_arrived(step):
-        n = pl.ds(0, step + 1)
-        arrived(hl.at[step, n], hr.at[step, n], h_sems, (step,))
-
     def node(level, slot, cs_ref, from_left, from_right, dst_right, dst_left):
         turn = turns(offs_ref, level)
         outside = jnp.logical_or(slot < 0, slot >= n_pair)
         swap = jnp.logical_or(jnp.logical_or(slot < -1, slot == 0), slot >= n_pair)
-        for g in range(level + 1):
-            at = pl.ds(g * WIDTH, WIDTH)
-            if level == 0:
-                row = lax.broadcasted_iota(jnp.int32, (WIDTH, B), 0)
-                col = lax.broadcasted_iota(jnp.int32, (WIDTH, B), 1)
-                f, s = [jnp.where(row == col + h, 1.0, 0.0).astype(F32) for h in (0, B)]
-            else:
-                zero = jnp.zeros((WIDTH, B), F32)
-                p = from_left[at, :] if g < level else zero
-                q = from_right[pl.ds((g - 1) * WIDTH, WIDTH), :] if g > 0 else zero
-                f, s = jnp.where(outside, q, p), jnp.where(outside, p, q)
-            f, s = rotated(f, s, cs_ref, turn)
-            if dst_right is not None:
-                dst_right[at, :] = jnp.where(swap, s, f)
-            if dst_left is not None:
-                dst_left[at, :] = jnp.where(swap, f, s)
-
-    total = jnp.zeros((WIDTH, WIDTH), F32)
-    for c in range(CHUNKS):
-        fetch[c].wait()
-        total = total + gram(x_in[pl.ds(c * chunk, chunk), :])
+        if level == 0:
+            row = lax.broadcasted_iota(jnp.int32, (WIDTH, B), 0)
+            col = lax.broadcasted_iota(jnp.int32, (WIDTH, B), 1)
+            f, s = [jnp.where(row == col + h, 1.0, 0.0).astype(F32) for h in (0, B)]
+        else:
+            zero = jnp.zeros((WIDTH, B), F32)
+            p = jnp.concatenate([from_left[...], zero], axis=0)
+            q = jnp.concatenate([zero, from_right[...]], axis=0)
+            f, s = jnp.where(outside, q, p), jnp.where(outside, p, q)
+        f, s = rotated(f, s, cs_ref, turn)
+        if dst_right is not None:
+            dst_right[...] = jnp.where(swap, s, f)
+        if dst_left is not None:
+            dst_left[...] = jnp.where(swap, f, s)
+
+    def rebuild(step):
+        if step == 1:
+            node(0, k - 1, hl.at[0, 0], None, None, r0l, l0l)
+            node(0, k + 1, hr.at[0, 0], None, None, r0r, l0r)
+        if step == 2:
+            node(1, k, cs.at[1], r0l, l0r, r1, l1)
+        if step == 3:
+            node(0, k - 3, hl.at[2, 0], None, None, edge0.at[0], None)
+            node(0, k + 3, hr.at[2, 0], None, None, None, edge0.at[1])
+            node(1, k - 2, hl.at[2, 1], edge0.at[0], l0l, edge1.at[0], None)
+            node(1, k + 2, hr.at[2, 1], r0r, edge0.at[1], None, edge1.at[1])
+            node(2, k - 1, hl.at[2, 2], edge1.at[0], l1, w3f, None)
+            node(2, k + 1, hr.at[2, 2], r1, edge1.at[1], None, w3s)
+
+    for copy in fetch:
+        copy.wait()
+    pl.semaphore_wait(barrier, n_row - 1 + (k > 0).astype(jnp.int32) + (k < n_pair - 1).astype(jnp.int32))
+    send_early(0)
+    total = gram(x_in[...])
     fetch_offs.wait()
     for step in range(STEPS):
-        if step > 0:
-            history_arrived(step - 1)
-            if step == 1:
-                node(0, k - 1, hl.at[0, 0], None, None, r0l, l0l)
-                node(0, k + 1, hr.at[0, 0], None, None, r0r, l0r)
-            if step == 2:
-                node(1, k, cs.at[1], r0l, l0r, r1, l1)
-            if step == 3:
-                node(0, k - 3, hl.at[2, 0], None, None, edge0, None)
-                node(1, k - 2, hl.at[2, 1], edge0, l0l, edge1, None)
-                node(2, k - 1, hl.at[2, 2], edge1, l1, w3f, None)
-                node(0, k + 3, hr.at[2, 0], None, None, None, edge0)
-                node(1, k + 2, hr.at[2, 1], r0r, edge0, None, edge1)
-                node(2, k + 1, hr.at[2, 2], r1, edge1, None, w3s)
-            total = jnp.zeros((WIDTH, WIDTH), F32)
-            for c in range(CHUNKS):
-                at = pl.ds(c * chunk, chunk)
-                arrived(xf.at[step - 1, at], xs.at[step - 1, at], x_sems, (step - 1, c))
-                total = total + gram(jnp.concatenate([xf[step - 1, at, :], xs[step - 1, at, :]], axis=1))
         pick_diagonals(total, w_ref, gs.at[step, me], offs_ref, step)
-        if step == 0:
-            pl.semaphore_wait(barrier, n_row - 1 + (k > 0).astype(jnp.int32) + (k < n_pair - 1).astype(jnp.int32))
         for j in range(1, n_row):
             peer_copy(step, me, lax.rem(me + j, n_row)).start()
+        rebuild(step)
         for j in range(1, n_row):
             peer_copy(step, lax.rem(me + j, n_row), lax.rem(me + j, n_row)).wait_recv()
         tot[...] = sum((gs[step, i] for i in range(1, n_row)), gs[step, 0])
         solve_angles(tot, offs_ref, step, cs.at[step])
+        if step == STEPS - 1:
+            break
         turn = turns(offs_ref, step)
-        if step < STEPS - 1:
-            send_history(step)
-        for c in range(CHUNKS):
-            at = pl.ds(c * chunk, chunk)
+        send_history(step)
+        for c in range(LATE):
+            at = late_rows(c)
             if step == 0:
                 f, s = x_in[at, :B], x_in[at, B:]
             else:
                 f, s = xf[step - 1, at, :], xs[step - 1, at, :]
             f, s = rotated(f, s, cs.at[step], turn)
-            if step < STEPS - 1:
-                of[step, at, :] = f
-                os_[step, at, :] = s
-                send_rows(step, c)
-            else:
-                x_out[at, :B] = f
-                x_out[at, B:] = s
+            of[step, at, :] = f
+            os_[step, at, :] = s
+            send_late(step, c)
+        n = pl.ds(0, step + 1)
+        arrived(hl.at[step, n], hr.at[step, n], h_sems, (step,))
+        for h in range(2):
+            arrived(el.at[step, h], er.at[step, h], e_sems, (step, h))
+        rotate_early(step)
+        total = gram(jnp.concatenate([xf[step, top, :], xs[step, top, :]], axis=1))
+        for c in range(LATE):
+            at = late_rows(c)
+            arrived(xf.at[step, at], xs.at[step, at], x_sems, (step, c))
+            if c == LATE - 1 and step + 1 < STEPS - 1:
+                send_early(step + 1)
+            total = total + gram(jnp.concatenate([xf[step, at, :], xs[step, at, :]], axis=1))
 
     turn = turns(offs_ref, STEPS - 1)
-    for g in range(STEPS):
-        at = pl.ds(g * WIDTH, WIDTH)
-        zero = jnp.zeros((WIDTH, B), F32)
-        f = w3f[at, :] if g < STEPS - 1 else zero
-        s = w3s[pl.ds((g - 1) * WIDTH, WIDTH), :] if g > 0 else zero
+    for g in range(2):
+        at = pl.ds(g * (rows // 2), rows // 2)
+        f, s = rotated(xf[STEPS - 2, at, :], xs[STEPS - 2, at, :], cs.at[STEPS - 1], turn)
+        x_out[at, :B] = f
+        x_out[at, B:] = s
+    zero = jnp.zeros((WIDTH, B), F32)
+    w_out_rows = [
+        (w3f[: 2 * WIDTH, :], jnp.concatenate([zero, w3s[:WIDTH, :]], axis=0)),
+        (jnp.concatenate([w3f[2 * WIDTH :, :], zero], axis=0), w3s[WIDTH:, :]),
+    ]
+    for g, (f, s) in enumerate(w_out_rows):
+        at = pl.ds(g * 2 * WIDTH, 2 * WIDTH)
         f, s = rotated(f, s, cs.at[STEPS - 1], turn)
         w_out[at, :B] = f
         w_out[at, B:] = s
@@ -326,8 +370,10 @@
         if step < STEPS - 1:
             n = pl.ds(0, step + 1)
             sent(le.at[step, n], re.at[step, n], h_sems, (step,))
-            for c in range(CHUNKS):
-                at = pl.ds(c * chunk, chunk)
+            for h in range(2):
+                sent(early_source(step, h), early_source(step, h), e_sems, (step, h))
+            for c in range(LATE):
+                at = late_rows(c)
                 sent(of.at[step, at], os_.at[step, at], x_sems, (step, c))
 
 
@@ -367,18 +413,20 @@
     rows, width = whitened.shape
     v_rows = n_pair * width // n_row
     blocks = v_rows // width
+    early = rows * EARLY // 16
     sds = functools.partial(jax.ShapeDtypeStruct, dtype=F32)
     vmem = pl.BlockSpec(memory_space=pltpu.VMEM)
     anywhere = pl.BlockSpec(memory_space=pl.ANY)
+    hbm = pl.BlockSpec(memory_space=pltpu.HBM)
     dma = pltpu.SemaphoreType.DMA
 
     def held(*shape):
         return pltpu.VMEM(shape, F32)
 
     x_last, w_last = pl.pallas_call(
-        functools.partial(main_kernel, n_pair, n_row, rows),
+        functools.partial(main_kernel, n_pair, n_row, rows, early),
         out_shape=[sds((rows, width)), sds((STEPS * width, width))],
-        in_specs=[anywhere, anywhere],
+        in_specs=[hbm, hbm],
         out_specs=[vmem, vmem],
         scratch_shapes=[
             pltpu.SMEM((STEPS, ROUNDS), jnp.int32),
@@ -387,32 +435,38 @@
             held(STEPS - 1, rows, B),
             held(STEPS - 1, rows, B),
             held(STEPS - 1, rows, B),
+            held(STEPS - 1, 2, early, B),
+            held(STEPS - 1, 2, early, B),
             held(4, B, B),
             held(STEPS, n_row, ROWS_SENT, B),
             held(ROWS_SENT, B),
             held(STEPS, 2 * ROUNDS, B),
         ]
         + [held(STEPS - 1, STEPS - 1, 2 * ROUNDS, B) for _ in range(4)]
-        + [held(n * width, B) for n in (1, 1, 1, 1, 2, 2, 1, 2, 3, 3)]
+        + [held(n * width, B) for n in (1, 1, 1, 1, 2, 2)]
+        + [held(2, width, B), held(2, 2 * width, B), held(3 * width, B), held(3 * width, B)]
         + [
-            dma((CHUNKS + 1,)),
+            dma((FETCHES + 1,)),
             dma((STEPS, n_row)),
             dma((STEPS, n_row)),
-            dma((2, STEPS - 1, CHUNKS)),
-            dma((2, STEPS - 1, CHUNKS)),
+            dma((2, STEPS - 1, LATE)),
+            dma((2, STEPS - 1, LATE)),
+            dma((2, STEPS - 1, 2)),
+            dma((2, STEPS - 1, 2)),
             dma((2, STEPS - 1)),
             dma((2, STEPS - 1)),
         ],
         compiler_params=pltpu.CompilerParams(
             collective_id=0, has_side_effects=True, vmem_limit_bytes=40 * 1024 * 1024
         ),
-    )(offsets, whitened)
+    )(pltpu.with_memory_space_constraint(offsets, pltpu.HBM), pltpu.with_memory_space_constraint(whitened, pltpu.HBM))
     return pl.pallas_call(
         functools.partial(place_kernel, n_pair, blocks),
         out_shape=[sds((rows, width)), sds((v_rows, width))],
         in_specs=[vmem, vmem],
         out_specs=[anywhere, anywhere],
         scratch_shapes=[held(width, width), dma((blocks + STEPS + 1,))],
+        compiler_params=pltpu.CompilerParams(vmem_limit_bytes=4 * 1024 * 1024),
     )(x_last, w_last)
 
 

time: 64.7 us -> 52.6 us (0.81)
  Pallas kernels: 59.8 us -> 51.7 us
  local copies, waits for them, and re-layouts: 3.87 us -> 0 us
    pallas_call x1, Pallas kernels: 55.8 us -> 49.2 us  [body(): pl.pallas_call(functools.partial(main_kernel, n_pair, n_row, rows, early)...]
    unnamed x8 -> x0, local copies, waits for them, and re-layouts: 3.87 us -> none
    pallas_call x1, Pallas kernels: 4.04 us -> 2.5 us  [body(): pl.pallas_call(functools.partial(place_kernel, n_pair, blocks), out_shape...]
where the time goes in v1:
time: 52.6 us; the launch traced here: 52.5 us
  Pallas kernels  51.7 us (98%)
  between operations  0.8 us (2%)
    pallas_call x1, Pallas kernels, body(): pl.pallas_call(functools.partial(main_kernel, n_pair, n_row, rows, early)...  49.2 us
    pallas_call x1, Pallas kernels, body(): pl.pallas_call(functools.partial(place_kernel, n_pair, blocks), out_shape...  2.5 us

profile of v1, /device:TPU:24, one launch (start us, length us, event | category | flops | bytes accessed | tf_op | source)
XLA Modules:
  0.0 52.5 jit_solution(2226317013379689294)
XLA Ops:
  0.6 49.2 %shard_map.41 = (f32[1024,256]{1,0:T(8,128)S(1)}, f32[1024,256]{1,0:T(8,128)S(1)}) custom-call(s32[4,4]{1,0:T(4,128)} %offs_hbm.1, f32[1024,256]{1,0:T(8,128)} %x_hbm.1), custom_call_target="tpu_custom_call" | custom-call | tf_op jit(solution)/shard_map/pallas_call | solution.py:426
  49.9 2.5 %shard_map.42 = (f32[1024,256]{1,0:T(8,128)}, f32[4096,256]{1,0:T(8,128)}) custom-call(f32[1024,256]{1,0:T(8,128)S(1)} %get-tuple-element.4.x_ref, f32[1024,256]{1,0:T(8,128)S(1)} %get-tuple-element.5.w_ref), custom_call_target="tpu_custom_call" | custom-call | tf_op jit(solution)/shard_map/pallas_call | solution.py:463

commit v2 on v1

--- a/solution.py
+++ b/solution.py
@@ -12,8 +12,8 @@
 ROUNDS = 4
 STEPS = 4
 FETCHES = 4
-LATE = 3
-EARLY = 7
+EARLY = (7, 12, 12)
+LATE = ((4, 6, 4, 4), (6, 2), (6, 2))
 SETS = 14
 ROWS_SENT = 4 * SETS
 MESH = pl.DeviceIdType.MESH
@@ -56,15 +56,19 @@
     w_ref[2] = total[:B, :B]
     w_ref[3] = total[B:, :B]
     base = lax.broadcasted_iota(jnp.int32, (8, B), 0) - lax.broadcasted_iota(jnp.int32, (8, B), 1)
-    for q in range(4):
-        at = [lax.rem(e - o + B, B) if q == 1 else lax.rem(e + o, B) if q == 3 else e for e in far[0]]
-        acc = [jnp.zeros((8, B), F32) for _ in at]
+    same, to_first, to_second = far[0], [lax.rem(e - o + B, B) for e in far[0]], [lax.rem(e + o, B) for e in far[0]]
+    for at, blocks in ((same, (0, 2)), (to_first, (1,)), (to_second, (3,))):
+        acc = [[jnp.zeros((8, B), F32) for _ in at] for _ in blocks]
         for g in range(B // 8):
-            m = w_ref[q, 8 * g : 8 * g + 8, :]
             dist = (base + 8 * g) & (B - 1)
-            acc = [jnp.where(dist == t, m, v) for t, v in zip(at, acc)]
-        for i, v in enumerate(acc):
-            dst_ref[pl.ds(q * SETS + i, 1), :] = jnp.sum(v, axis=0, keepdims=True)
+            m = [w_ref[q, 8 * g : 8 * g + 8, :] for q in blocks]
+            for i, t in enumerate(at):
+                here = dist == t
+                for n in range(len(blocks)):
+                    acc[n][i] = jnp.where(here, m[n], acc[n][i])
+        for n, q in enumerate(blocks):
+            for i, v in enumerate(acc[n]):
+                dst_ref[pl.ds(q * SETS + i, 1), :] = jnp.sum(v, axis=0, keepdims=True)
     dst_ref[pl.ds(0, 2 * SETS), :] = ahead(dst_ref[pl.ds(0, 2 * SETS), :], o)
 
 
@@ -119,17 +123,20 @@
 
 
 def main_kernel(
-    n_pair, n_row, rows, early, offs_hbm, x_hbm, x_out, w_out,
+    n_pair, n_row, rows, early, offs_hbm, x_hbm, x3f, x3s, w3f, w3s, cs_out, turn_out,
     offs_ref, x_in, xf, xs, of, os_, el, er, w_ref, gs, tot, cs, hl, hr, le, re,
-    r0l, l0l, r0r, l0r, r1, l1, edge0, edge1, w3f, w3s,
+    r0l, l0l, r0r, l0r, r1, l1, edge0, edge1,
     in_sem, g_send, g_recv, x_send, x_recv, e_send, e_recv, h_send, h_recv,
 ):
     k = lax.axis_index("pair")
     me = lax.axis_index("row")
     first, last = k == 0, k == n_pair - 1
     piece = rows // FETCHES
-    late = (rows - early) // LATE
-    top = pl.ds(0, early)
+    late = []
+    for n, sizes in zip(early, LATE):
+        ends = [n + sum(sizes[: i + 1]) * (rows // 32) for i in range(len(sizes))]
+        late.append([(end - size * (rows // 32), size * (rows // 32)) for end, size in zip(ends, sizes)])
+    parts = [[(0, early[0])]] + [[(0, a)] + [(a, b - a)] * (b > a) for a, b in zip(early, early[1:])]
 
     fetch_offs = pltpu.make_async_copy(offs_hbm, offs_ref, in_sem.at[FETCHES])
     fetch_offs.start()
@@ -191,13 +198,18 @@
 
     x_sems, e_sems, h_sems = (x_send, x_recv), (e_send, e_recv), (h_send, h_recv)
 
-    def late_rows(c):
-        return pl.ds(early + c * late, late)
+    def new(h, step):
+        if step == STEPS - 2:
+            return (x3f, x3s)[h]
+        return (xf, xs)[h].at[step]
+
+    def late_rows(step, c):
+        return pl.ds(*late[step][c])
 
     def send_late(step, c):
-        at = late_rows(c)
+        at = late_rows(step, c)
         f, s = of.at[step, at], os_.at[step, at]
-        new_f, new_s = xf.at[step, at], xs.at[step, at]
+        new_f, new_s = new(0, step).at[at], new(1, step).at[at]
 
         @pl.when(first)
         def _():
@@ -216,37 +228,63 @@
         def _():
             to_left(s, new_s, x_sems, (step, c)).start()
 
-    def early_source(step, h):
-        if step == 0:
-            return x_in.at[top, pl.ds(h * B, B)]
-        return (xf, xs)[h].at[step - 1, top]
-
-    def send_early(step):
+    def early_moves(step, part):
+        at = pl.ds(*parts[step][part])
         for h in range(2):
-            src = early_source(step, h)
+            if step == 0:
+                src = x_in.at[at, pl.ds(h * B, B)]
+                yield h, src, src, el.at[step, h, at], er.at[step, h, at]
+            elif h == 0:
+                yield h, new(0, step - 1).at[at], new(1, step - 1).at[at], el.at[step, 0, at], er.at[step, 1, at]
+
+    def send_early(step, part):
+        for h, to_r, to_l, from_l, from_r in early_moves(step, part):
 
             @pl.when(k < n_pair - 1)
             def _():
-                to_right(src, el.at[step, h], e_sems, (step, h)).start()
+                to_right(to_r, from_l, e_sems, (step, h, part)).start()
 
             @pl.when(k > 0)
             def _():
-                to_left(src, er.at[step, h], e_sems, (step, h)).start()
-
-            @pl.when(first)
-            def _():
-                el[step, h] = src[...]
-
-            @pl.when(last)
-            def _():
-                er[step, h] = src[...]
+                to_left(to_l, from_r, e_sems, (step, h, part)).start()
+
+        at = pl.ds(*parts[step][part])
+        own = [x_in.at[at, pl.ds(h * B, B)] if step == 0 else new(h, step - 1).at[at] for h in range(2)]
+
+        @pl.when(first)
+        def _():
+            for h in range(2):
+                el[step, h, at] = own[h][...]
+
+        @pl.when(last)
+        def _():
+            for h in range(2):
+                er[step, h, at] = own[h][...]
+
+    def rotate_own_early(step):
+        top = pl.ds(0, early[step])
+        if step == 0:
+            f, s = x_in[top, :B], x_in[top, B:]
+        else:
+            f, s = xf[step - 1, top, :], xs[step - 1, top, :]
+        of[step, top, :], os_[step, top, :] = rotated(f, s, cs.at[step], turns(offs_ref, step))
 
     def rotate_early(step):
+        top = pl.ds(0, early[step])
+        for part in range(len(parts[step])):
+            for h, _, _, from_l, from_r in early_moves(step, part):
+                arrived(from_l, from_r, e_sems, (step, h, part))
         turn = turns(offs_ref, step)
-        f, s = rotated(el[step, 0], el[step, 1], hl.at[step, step], turn)
-        xf[step, top, :] = jnp.where(k == 1, s, f)
-        f, s = rotated(er[step, 0], er[step, 1], hr.at[step, step], turn)
-        xs[step, top, :] = jnp.where(last, f, s)
+        f, s = el[step, 0, top], el[step, 1, top]
+        if step > 0:
+            s = jnp.where(first, s, os_[step - 1, top, :])
+        f, s = rotated(f, s, hl.at[step, step], turn)
+        new(0, step)[top, :] = jnp.where(k == 1, s, f)
+        f, s = er[step, 0, top], er[step, 1, top]
+        if step > 0:
+            f = jnp.where(last, f, jnp.where(first, os_[step - 1, top, :], of[step - 1, top, :]))
+        f, s = rotated(f, s, hr.at[step, step], turn)
+        new(1, step)[top, :] = jnp.where(last, f, s)
 
     def send_history(step):
         if step > 0:
@@ -305,16 +343,22 @@
             node(2, k - 1, hl.at[2, 2], edge1.at[0], l1, w3f, None)
             node(2, k + 1, hr.at[2, 2], r1, edge1.at[1], None, w3s)
 
-    for copy in fetch:
-        copy.wait()
+    total = jnp.zeros((WIDTH, WIDTH), F32)
+    for c in range(FETCHES // 2):
+        fetch[c].wait()
+        total = total + gram(x_in[pl.ds(c * piece, piece), :])
     pl.semaphore_wait(barrier, n_row - 1 + (k > 0).astype(jnp.int32) + (k < n_pair - 1).astype(jnp.int32))
-    send_early(0)
-    total = gram(x_in[...])
+    send_early(0, 0)
+    for c in range(FETCHES // 2, FETCHES):
+        fetch[c].wait()
+        total = total + gram(x_in[pl.ds(c * piece, piece), :])
     fetch_offs.wait()
     for step in range(STEPS):
         pick_diagonals(total, w_ref, gs.at[step, me], offs_ref, step)
         for j in range(1, n_row):
             peer_copy(step, me, lax.rem(me + j, n_row)).start()
+        if 0 < step < STEPS - 1:
+            rotate_own_early(step - 1)
         rebuild(step)
         for j in range(1, n_row):
             peer_copy(step, lax.rem(me + j, n_row), lax.rem(me + j, n_row)).wait_recv()
@@ -324,8 +368,8 @@
             break
         turn = turns(offs_ref, step)
         send_history(step)
-        for c in range(LATE):
-            at = late_rows(c)
+        for c in range(len(late[step])):
+            at = late_rows(step, c)
             if step == 0:
                 f, s = x_in[at, :B], x_in[at, B:]
             else:
@@ -336,33 +380,25 @@
             send_late(step, c)
         n = pl.ds(0, step + 1)
         arrived(hl.at[step, n], hr.at[step, n], h_sems, (step,))
-        for h in range(2):
-            arrived(el.at[step, h], er.at[step, h], e_sems, (step, h))
         rotate_early(step)
-        total = gram(jnp.concatenate([xf[step, top, :], xs[step, top, :]], axis=1))
-        for c in range(LATE):
-            at = late_rows(c)
-            arrived(xf.at[step, at], xs.at[step, at], x_sems, (step, c))
-            if c == LATE - 1 and step + 1 < STEPS - 1:
-                send_early(step + 1)
-            total = total + gram(jnp.concatenate([xf[step, at, :], xs[step, at, :]], axis=1))
-
-    turn = turns(offs_ref, STEPS - 1)
-    for g in range(2):
-        at = pl.ds(g * (rows // 2), rows // 2)
-        f, s = rotated(xf[STEPS - 2, at, :], xs[STEPS - 2, at, :], cs.at[STEPS - 1], turn)
-        x_out[at, :B] = f
-        x_out[at, B:] = s
-    zero = jnp.zeros((WIDTH, B), F32)
-    w_out_rows = [
-        (w3f[: 2 * WIDTH, :], jnp.concatenate([zero, w3s[:WIDTH, :]], axis=0)),
-        (jnp.concatenate([w3f[2 * WIDTH :, :], zero], axis=0), w3s[WIDTH:, :]),
-    ]
-    for g, (f, s) in enumerate(w_out_rows):
-        at = pl.ds(g * 2 * WIDTH, 2 * WIDTH)
-        f, s = rotated(f, s, cs.at[STEPS - 1], turn)
-        w_out[at, :B] = f
-        w_out[at, B:] = s
+        if step + 1 < STEPS - 1:
+            send_early(step + 1, 0)
+        top = pl.ds(0, early[step])
+        total = gram(jnp.concatenate([new(h, step)[top, :] for h in range(2)], axis=1))
+        for c in range(len(late[step])):
+            at = late_rows(step, c)
+            arrived(new(0, step).at[at], new(1, step).at[at], x_sems, (step, c))
+            if step + 1 < STEPS - 1 and len(parts[step + 1]) > 1 and sum(late[step][c]) == early[step + 1]:
+                send_early(step + 1, 1)
+            total = total + gram(jnp.concatenate([new(h, step)[at, :] for h in range(2)], axis=1))
+
+    cs_out[...] = cs[STEPS - 1]
+    shifts, back = turns(offs_ref, STEPS - 1)
+    row = lax.broadcasted_iota(jnp.int32, (2 * ROUNDS, B), 0)
+    table = jnp.full((2 * ROUNDS, B), back, jnp.int32)
+    for r in range(ROUNDS):
+        table = jnp.where(row == r, shifts[r], table)
+    turn_out[...] = table
 
     for step in range(STEPS):
         for j in range(1, n_row):
@@ -370,17 +406,17 @@
         if step < STEPS - 1:
             n = pl.ds(0, step + 1)
             sent(le.at[step, n], re.at[step, n], h_sems, (step,))
-            for h in range(2):
-                sent(early_source(step, h), early_source(step, h), e_sems, (step, h))
-            for c in range(LATE):
-                at = late_rows(c)
+            for part in range(len(parts[step])):
+                for h, to_r, to_l, _, _ in early_moves(step, part):
+                    sent(to_r, to_l, e_sems, (step, h, part))
+            for c in range(len(late[step])):
+                at = late_rows(step, c)
                 sent(of.at[step, at], os_.at[step, at], x_sems, (step, c))
 
 
-def place_kernel(n_pair, blocks, x_ref, w_ref, x_out, v_out, zero, sem):
+def place_kernel(n_pair, blocks, turn_ref, cs_ref, xf, xs, wf, ws, x_out, v_out, x_last, w_last, zero, sem):
     k, me = lax.axis_index("pair"), lax.axis_index("row")
-    move_x = pltpu.make_async_copy(x_ref, x_out, sem.at[blocks + STEPS])
-    move_x.start()
+    half = xf.shape[0] // 2
     zero[...] = jnp.zeros_like(zero)
     slots = []
     for j in range(STEPS):
@@ -392,7 +428,7 @@
         here = jnp.logical_and(slots[j] >= 0, slots[j] < blocks)
         place = pl.multiple_of(jnp.where(here, slots[j], 0) * WIDTH, WIDTH)
         return here, pltpu.make_async_copy(
-            w_ref.at[pl.ds(j * WIDTH, WIDTH)], v_out.at[pl.ds(place, WIDTH)], sem.at[blocks + j]
+            w_last.at[pl.ds(j * WIDTH, WIDTH)], v_out.at[pl.ds(place, WIDTH)], sem.at[blocks + j]
         )
 
     def blank(b):
@@ -401,19 +437,41 @@
             empty = jnp.logical_and(empty, slots[j] != b)
         return empty, pltpu.make_async_copy(zero, v_out.at[pl.ds(b * WIDTH, WIDTH)], sem.at[b])
 
-    moves = [piece(j) for j in range(STEPS)] + [blank(b) for b in range(blocks)]
-    for needed, copy in moves:
+    pieces, blanks = [piece(j) for j in range(STEPS)], [blank(b) for b in range(blocks)]
+    for needed, copy in blanks:
         pl.when(needed)(copy.start)
-    for needed, copy in moves:
+    turn = [turn_ref[r, 0] for r in range(ROUNDS)], turn_ref[ROUNDS, 0]
+    moves = []
+    for g in range(2):
+        at = pl.ds(g * half, half)
+        f, s = rotated(xf[at, :], xs[at, :], cs_ref, turn)
+        x_last[at, :B] = f
+        x_last[at, B:] = s
+        moves.append(pltpu.make_async_copy(x_last.at[at], x_out.at[at], sem.at[blocks + STEPS + g]))
+        moves[-1].start()
+    blank_rows = jnp.zeros((WIDTH, B), F32)
+    parts = [
+        (wf[: 2 * WIDTH, :], jnp.concatenate([blank_rows, ws[:WIDTH, :]], axis=0)),
+        (jnp.concatenate([wf[2 * WIDTH :, :], blank_rows], axis=0), ws[WIDTH:, :]),
+    ]
+    for g, (f, s) in enumerate(parts):
+        at = pl.ds(g * 2 * WIDTH, 2 * WIDTH)
+        f, s = rotated(f, s, cs_ref, turn)
+        w_last[at, :B] = f
+        w_last[at, B:] = s
+        for needed, copy in pieces[2 * g : 2 * g + 2]:
+            pl.when(needed)(copy.start)
+    for needed, copy in pieces + blanks:
         pl.when(needed)(copy.wait)
-    move_x.wait()
+    for copy in moves:
+        copy.wait()
 
 
 def body(n_pair, n_row, whitened, offsets):
     rows, width = whitened.shape
     v_rows = n_pair * width // n_row
     blocks = v_rows // width
-    early = rows * EARLY // 16
+    early = [rows * n // 16 for n in EARLY]
     sds = functools.partial(jax.ShapeDtypeStruct, dtype=F32)
     vmem = pl.BlockSpec(memory_space=pltpu.VMEM)
     anywhere = pl.BlockSpec(memory_space=pl.ANY)
@@ -423,20 +481,22 @@
     def held(*shape):
         return pltpu.VMEM(shape, F32)
 
-    x_last, w_last = pl.pallas_call(
+    *held_rows, cs, turn = pl.pallas_call(
         functools.partial(main_kernel, n_pair, n_row, rows, early),
-        out_shape=[sds((rows, width)), sds((STEPS * width, width))],
+        out_shape=[sds((rows, B))] * 2
+        + [sds(((STEPS - 1) * width, B))] * 2
+        + [sds((2 * ROUNDS, B)), jax.ShapeDtypeStruct((2 * ROUNDS, B), jnp.int32)],
         in_specs=[hbm, hbm],
-        out_specs=[vmem, vmem],
+        out_specs=[vmem] * 6,
         scratch_shapes=[
             pltpu.SMEM((STEPS, ROUNDS), jnp.int32),
             held(rows, width),
+            held(STEPS - 2, rows, B),
+            held(STEPS - 2, rows, B),
             held(STEPS - 1, rows, B),
             held(STEPS - 1, rows, B),
-            held(STEPS - 1, rows, B),
-            held(STEPS - 1, rows, B),
-            held(STEPS - 1, 2, early, B),
-            held(STEPS - 1, 2, early, B),
+            held(STEPS - 1, 2, max(early), B),
+            held(STEPS - 1, 2, max(early), B),
             held(4, B, B),
             held(STEPS, n_row, ROWS_SENT, B),
             held(ROWS_SENT, B),
@@ -444,15 +504,15 @@
         ]
         + [held(STEPS - 1, STEPS - 1, 2 * ROUNDS, B) for _ in range(4)]
         + [held(n * width, B) for n in (1, 1, 1, 1, 2, 2)]
-        + [held(2, width, B), held(2, 2 * width, B), held(3 * width, B), held(3 * width, B)]
+        + [held(2, width, B), held(2, 2 * width, B)]
         + [
             dma((FETCHES + 1,)),
             dma((STEPS, n_row)),
             dma((STEPS, n_row)),
-            dma((2, STEPS - 1, LATE)),
-            dma((2, STEPS - 1, LATE)),
-            dma((2, STEPS - 1, 2)),
-            dma((2, STEPS - 1, 2)),
+            dma((2, STEPS - 1, max(map(len, LATE)))),
+            dma((2, STEPS - 1, max(map(len, LATE)))),
+            dma((2, STEPS - 1, 2, 2)),
+            dma((2, STEPS - 1, 2, 2)),
             dma((2, STEPS - 1)),
             dma((2, STEPS - 1)),
         ],
@@ -463,11 +523,11 @@
     return pl.pallas_call(
         functools.partial(place_kernel, n_pair, blocks),
         out_shape=[sds((rows, width)), sds((v_rows, width))],
-        in_specs=[vmem, vmem],
+        in_specs=[vmem] * 6,
         out_specs=[anywhere, anywhere],
-        scratch_shapes=[held(width, width), dma((blocks + STEPS + 1,))],
-        compiler_params=pltpu.CompilerParams(vmem_limit_bytes=4 * 1024 * 1024),
-    )(x_last, w_last)
+        scratch_shapes=[held(rows, width), held(STEPS * width, width), held(width, width), dma((blocks + STEPS + 2,))],
+        compiler_params=pltpu.CompilerParams(vmem_limit_bytes=8 * 1024 * 1024),
+    )(turn, cs, *held_rows)
 
 
 def solution(mesh):

time: 52.6 us -> 51.1 us (0.971)
  Pallas kernels: 51.7 us -> 50.2 us
    pallas_call x1, Pallas kernels: 49.2 us -> 47 us  [body(): pl.pallas_call(functools.partial(main_kernel, n_pair, n_row, rows, early)...]
    pallas_call x1, Pallas kernels: 2.5 us -> 3.15 us  [body(): pl.pallas_call(functools.partial(place_kernel, n_pair, blocks), out_shape...]
where the time goes in v2:
time: 51.1 us; the launch traced here: 51 us
  Pallas kernels  50.2 us (98%)
  between operations  0.8 us (2%)
    pallas_call x1, Pallas kernels, body(): pl.pallas_call(functools.partial(main_kernel, n_pair, n_row, rows, early)...  47 us
    pallas_call x1, Pallas kernels, body(): pl.pallas_call(functools.partial(place_kernel, n_pair, blocks), out_shape...  3.15 us

profile of v2, /device:TPU:24, one launch (start us, length us, event | category | flops | bytes accessed | tf_op | source)
XLA Modules:
  0.0 51.0 jit_solution(16012328077741196642)
XLA Ops:
  0.6 47.0 %shard_map.41 = (f32[1024,128]{1,0:T(8,128)S(1)}, f32[1024,128]{1,0:T(8,128)S(1)}, f32[768,128]{1,0:T(8,128)S(1)}, f32[768,128]{1,0:T(8,128)S(1)}, f32[8,128]{1,0:T(8,128)S(1)}, /*index=5*/s32[8,128]{1,0:T(8,128)S(1)}) custom-call(s32[4,4]{1,0:T(4,128)} %offs_hbm.1, f32[1024,256]{1,0:T(8,128)} %x_hbm.1), custom_call_target="tpu_custom_call" | custom-call | tf_op jit(solution)/shard_map/pallas_call | solution.py:484
  47.7 3.2 %shard_map.42 = (f32[1024,256]{1,0:T(8,128)}, f32[4096,256]{1,0:T(8,128)}) custom-call(s32[8,128]{1,0:T(8,128)S(1)} %get-tuple-element.8.turn_ref, f32[8,128]{1,0:T(8,128)S(1)} %get-tuple-element.9.cs_ref, f32[1024,128]{1,0:T(8,128)S(1)} %get-tuple-element.10.xf, f32[1024,128]{1,0:T(8,128)S(1)} %get-tuple-element.11.xs, ...), custom_call_target="tpu_custom_call" | custom-call | tf_op jit(solution)/shard_map/pallas_call | solution.py:523

commit v3 on v2

--- a/solution.py
+++ b/solution.py
@@ -13,6 +13,7 @@
 STEPS = 4
 FETCHES = 4
 EARLY = (7, 12, 12)
+TILES = (2, 3, 3)
 LATE = ((4, 6, 4, 4), (6, 2), (6, 2))
 SETS = 14
 ROWS_SENT = 4 * SETS
@@ -248,18 +249,23 @@
             def _():
                 to_left(to_l, from_r, e_sems, (step, h, part)).start()
 
-        at = pl.ds(*parts[step][part])
-        own = [x_in.at[at, pl.ds(h * B, B)] if step == 0 else new(h, step - 1).at[at] for h in range(2)]
+    def keep_own(step):
+        top = pl.ds(0, early[step])
+        own = [x_in.at[top, pl.ds(h * B, B)] if step == 0 else new(h, step - 1).at[top] for h in range(2)]
 
         @pl.when(first)
         def _():
             for h in range(2):
-                el[step, h, at] = own[h][...]
+                el[step, h, top] = own[h][...]
 
         @pl.when(last)
         def _():
             for h in range(2):
-                er[step, h, at] = own[h][...]
+                er[step, h, top] = own[h][...]
+
+    def hold(step, at, f, s):
+        el[step + 1, 1, at] = s
+        er[step + 1, 0, at] = jnp.where(first, s, f)
 
     def rotate_own_early(step):
         top = pl.ds(0, early[step])
@@ -267,24 +273,26 @@
             f, s = x_in[top, :B], x_in[top, B:]
         else:
             f, s = xf[step - 1, top, :], xs[step - 1, top, :]
-        of[step, top, :], os_[step, top, :] = rotated(f, s, cs.at[step], turns(offs_ref, step))
-
-    def rotate_early(step):
-        top = pl.ds(0, early[step])
+        f, s = rotated(f, s, cs.at[step], turns(offs_ref, step))
+        hold(step, top, f, s)
+
+    def early_gram(step):
         for part in range(len(parts[step])):
             for h, _, _, from_l, from_r in early_moves(step, part):
                 arrived(from_l, from_r, e_sems, (step, h, part))
         turn = turns(offs_ref, step)
-        f, s = el[step, 0, top], el[step, 1, top]
-        if step > 0:
-            s = jnp.where(first, s, os_[step - 1, top, :])
-        f, s = rotated(f, s, hl.at[step, step], turn)
-        new(0, step)[top, :] = jnp.where(k == 1, s, f)
-        f, s = er[step, 0, top], er[step, 1, top]
-        if step > 0:
-            f = jnp.where(last, f, jnp.where(first, os_[step - 1, top, :], of[step - 1, top, :]))
-        f, s = rotated(f, s, hr.at[step, step], turn)
-        new(1, step)[top, :] = jnp.where(last, f, s)
+        tile = early[step] // TILES[step]
+        total = jnp.zeros((WIDTH, WIDTH), F32)
+        for c in range(TILES[step]):
+            at = pl.ds(c * tile, tile)
+            f, s = rotated(el[step, 0, at], el[step, 1, at], hl.at[step, step], turn)
+            new_f = jnp.where(k == 1, s, f)
+            f, s = rotated(er[step, 0, at], er[step, 1, at], hr.at[step, step], turn)
+            new_s = jnp.where(last, f, s)
+            new(0, step)[at, :] = new_f
+            new(1, step)[at, :] = new_s
+            total = total + gram(jnp.concatenate([new_f, new_s], axis=1))
+        return total
 
     def send_history(step):
         if step > 0:
@@ -349,6 +357,7 @@
         total = total + gram(x_in[pl.ds(c * piece, piece), :])
     pl.semaphore_wait(barrier, n_row - 1 + (k > 0).astype(jnp.int32) + (k < n_pair - 1).astype(jnp.int32))
     send_early(0, 0)
+    keep_own(0)
     for c in range(FETCHES // 2, FETCHES):
         fetch[c].wait()
         total = total + gram(x_in[pl.ds(c * piece, piece), :])
@@ -359,6 +368,7 @@
             peer_copy(step, me, lax.rem(me + j, n_row)).start()
         if 0 < step < STEPS - 1:
             rotate_own_early(step - 1)
+            keep_own(step)
         rebuild(step)
         for j in range(1, n_row):
             peer_copy(step, lax.rem(me + j, n_row), lax.rem(me + j, n_row)).wait_recv()
@@ -378,13 +388,13 @@
             of[step, at, :] = f
             os_[step, at, :] = s
             send_late(step, c)
+            if step + 1 < STEPS - 1 and sum(late[step][c]) <= early[step + 1]:
+                hold(step, at, f, s)
         n = pl.ds(0, step + 1)
         arrived(hl.at[step, n], hr.at[step, n], h_sems, (step,))
-        rotate_early(step)
+        total = early_gram(step)
         if step + 1 < STEPS - 1:
             send_early(step + 1, 0)
-        top = pl.ds(0, early[step])
-        total = gram(jnp.concatenate([new(h, step)[top, :] for h in range(2)], axis=1))
         for c in range(len(late[step])):
             at = late_rows(step, c)
             arrived(new(0, step).at[at], new(1, step).at[at], x_sems, (step, c))

time: 51.1 us -> 49.5 us (0.969)
  Pallas kernels: 50.2 us -> 48.6 us
    pallas_call x1, Pallas kernels: 47 us -> 45.4 us  [body(): pl.pallas_call(functools.partial(main_kernel, n_pair, n_row, rows, early)...]
where the time goes in v3:
time: 49.5 us; the launch traced here: 49.4 us
  Pallas kernels  48.6 us (98%)
  between operations  0.8 us (2%)
    pallas_call x1, Pallas kernels, body(): pl.pallas_call(functools.partial(main_kernel, n_pair, n_row, rows, early)...  45.4 us
    pallas_call x1, Pallas kernels, body(): pl.pallas_call(functools.partial(place_kernel, n_pair, blocks), out_shape...  3.15 us

profile of v3, /device:TPU:24, one launch (start us, length us, event | category | flops | bytes accessed | tf_op | source)
XLA Modules:
  0.0 49.4 jit_solution(386075670975210457)
XLA Ops:
  0.6 45.4 %shard_map.41 = (f32[1024,128]{1,0:T(8,128)S(1)}, f32[1024,128]{1,0:T(8,128)S(1)}, f32[768,128]{1,0:T(8,128)S(1)}, f32[768,128]{1,0:T(8,128)S(1)}, f32[8,128]{1,0:T(8,128)S(1)}, /*index=5*/s32[8,128]{1,0:T(8,128)S(1)}) custom-call(s32[4,4]{1,0:T(4,128)} %offs_hbm.1, f32[1024,256]{1,0:T(8,128)} %x_hbm.1), custom_call_target="tpu_custom_call" | custom-call | tf_op jit(solution)/shard_map/pallas_call | solution.py:494
  46.1 3.2 %shard_map.42 = (f32[1024,256]{1,0:T(8,128)}, f32[4096,256]{1,0:T(8,128)}) custom-call(s32[8,128]{1,0:T(8,128)S(1)} %get-tuple-element.8.turn_ref, f32[8,128]{1,0:T(8,128)S(1)} %get-tuple-element.9.cs_ref, f32[1024,128]{1,0:T(8,128)S(1)} %get-tuple-element.10.xf, f32[1024,128]{1,0:T(8,128)S(1)} %get-tuple-element.11.xs, ...), custom_call_target="tpu_custom_call" | custom-call | tf_op jit(solution)/shard_map/pallas_call | solution.py:533

commit v4 on v3

--- a/solution.py
+++ b/solution.py
@@ -82,7 +82,7 @@
         radius = jnp.sqrt(gap * gap + c0 * c0)
         sign = jnp.where(gap >= 0, 1.0, -1.0)
         t = -sign * c0 / (jnp.abs(gap) + radius + 1e-06 * (a[0] + d[0]))
-        c = 1.0 / jnp.sqrt(1.0 + t * t)
+        c = lax.rsqrt(1.0 + t * t)
         s = t * c
         cs_ref[pl.ds(r, 1), :] = c
         cs_ref[pl.ds(ROUNDS + r, 1), :] = s
@@ -364,7 +364,7 @@
     fetch_offs.wait()
     for step in range(STEPS):
         pick_diagonals(total, w_ref, gs.at[step, me], offs_ref, step)
-        for j in range(1, n_row):
+        for j in sorted(range(1, n_row), key=lambda j: -min(j, n_row - j)):
             peer_copy(step, me, lax.rem(me + j, n_row)).start()
         if 0 < step < STEPS - 1:
             rotate_own_early(step - 1)

time: 49.5 us -> 48.8 us (0.986)
  Pallas kernels: 48.6 us -> 47.9 us
    pallas_call x1, Pallas kernels: 45.4 us -> 44.8 us  [body(): pl.pallas_call(functools.partial(main_kernel, n_pair, n_row, rows, early)...]
where the time goes in v4:
time: 48.8 us; the launch traced here: 48.7 us
  Pallas kernels  47.9 us (98%)
  between operations  0.8 us (2%)
    pallas_call x1, Pallas kernels, body(): pl.pallas_call(functools.partial(main_kernel, n_pair, n_row, rows, early)...  44.8 us
    pallas_call x1, Pallas kernels, body(): pl.pallas_call(functools.partial(place_kernel, n_pair, blocks), out_shape...  3.15 us

profile of v4, /device:TPU:24, one launch (start us, length us, event | category | flops | bytes accessed | tf_op | source)
XLA Modules:
  0.0 48.7 jit_solution(9243216324891782783)
XLA Ops:
  0.6 44.8 %shard_map.41 = (f32[1024,128]{1,0:T(8,128)S(1)}, f32[1024,128]{1,0:T(8,128)S(1)}, f32[768,128]{1,0:T(8,128)S(1)}, f32[768,128]{1,0:T(8,128)S(1)}, f32[8,128]{1,0:T(8,128)S(1)}, /*index=5*/s32[8,128]{1,0:T(8,128)S(1)}) custom-call(s32[4,4]{1,0:T(4,128)} %offs_hbm.1, f32[1024,256]{1,0:T(8,128)} %x_hbm.1), custom_call_target="tpu_custom_call" | custom-call | tf_op jit(solution)/shard_map/pallas_call | solution.py:494
  45.4 3.2 %shard_map.42 = (f32[1024,256]{1,0:T(8,128)}, f32[4096,256]{1,0:T(8,128)}) custom-call(s32[8,128]{1,0:T(8,128)S(1)} %get-tuple-element.8.turn_ref, f32[8,128]{1,0:T(8,128)S(1)} %get-tuple-element.9.cs_ref, f32[1024,128]{1,0:T(8,128)S(1)} %get-tuple-element.10.xf, f32[1024,128]{1,0:T(8,128)S(1)} %get-tuple-element.11.xs, ...), custom_call_target="tpu_custom_call" | custom-call | tf_op jit(solution)/shard_map/pallas_call | solution.py:533
